TPU v7x, 32 devices: a whole 2x2x4 slice. The times are simulated.
32 devices in a mesh: dp: 2 (over x), node: 4 (over z), local: 4 (over y, core).
Axes of the slice: x: 2, y: 2, z: 4, core: 2. Of those that a mesh axis runs over, the one named last changes fastest.
Arguments:
- tokens: bfloat16 [6144, 2048], P(('dp', 'node', 'local')), may hold values from -6 to 6
- cotangent: bfloat16 [6144, 2048], P(('dp', 'node', 'local')), may hold values from -6 to 6
- expert_of: int32 [6144, 1], P(('dp', 'node', 'local')), may hold values from 0 to 3; in each aligned block of 192 rows (0 to 191, 192 to 383, ...) at most 60 rows name the same one
- w1_codes: bfloat16 [4, 2048, 512], P('local', 'node'), may hold values from -4 to 4
- w1_scales: bfloat16 [4, 64, 512], P('local', 'node'), may hold values from 0.010986328 to 0.044921875
Outputs:
- grad_w2: bfloat16 [4, 2048, 512], P('local', 'node')
Inputs may be any that keep to these rules, and one draw needn't show every extreme that they name: `expert_of`: within the rows of one device (aligned blocks of 192 rows) no expert is named by more than 60 rows, a bound that some block reaches.
All inputs are finite; a program needn't handle non-finite values.
Results may differ from a plain program's by a relative error of at most 0.018.
Values may be sent and summed in bfloat16 or wider, within the bound.
No kernel may reach another device: no remote copies, remote signals or barrier semaphores. Data moves between devices by JAX's collectives and lax.ppermute only.
A program may use at most 64 MiB of HBM per device.

v0:
```python
import jax
import jax.numpy as jnp
from jax import lax
from jax.sharding import PartitionSpec as P

QB = 32


def slot_of(expert_ids, experts, capacity):
    chosen = expert_ids[:, 0]
    onehot = (chosen[:, None] == jnp.arange(experts, dtype=jnp.int32)[None, :]).astype(jnp.int32)
    ranking = jnp.sum((jnp.cumsum(onehot, axis=0) - 1) * onehot, axis=1)
    return chosen * capacity + ranking


def place(row_data, slots, experts, capacity):
    blank_rows = jnp.zeros((experts * capacity, row_data.shape[1]), row_data.dtype)
    return blank_rows.at[slots].set(row_data).reshape(experts, capacity, row_data.shape[1])


def dequant_piece(piece_codes, piece_scales):
    product = piece_codes.astype(jnp.float32) * piece_scales[:, None, :].astype(jnp.float32)
    return product.astype(jnp.bfloat16).reshape(piece_codes.shape[0] * QB, piece_codes.shape[2])


def contract_rows(left_rows, right_rows):
    return lax.dot_general(
        left_rows, right_rows, (((0,), (0,)), ((), ())), preferred_element_type=jnp.float32
    )


def on_device(tokens, cotangent, expert_of, w1_codes, w1_scales):
    experts = lax.axis_size("local")
    tok_dev = tokens.shape[0]
    features = tokens.shape[1]
    capacity = 5 * tok_dev // (4 * experts)
    slots = slot_of(expert_of, experts, capacity)
    sent_x = place(tokens, slots, experts, capacity)
    sent_dy = place(cotangent, slots, experts, capacity)
    got_x, got_dy = (
        lax.all_to_all(sent_x, "local", split_axis=0, concat_axis=0, tiled=True),
        lax.all_to_all(sent_dy, "local", split_axis=0, concat_axis=0, tiled=True),
    )
    served = experts * capacity
    rows_x = got_x.reshape(served, features)
    rows_dy = got_dy.reshape(served, features)
    hidden = w1_codes.shape[2]
    shard_rows = w1_codes.shape[1]
    blocks = shard_rows // QB
    code_up = w1_codes.reshape(blocks, QB, hidden)
    scale_up = w1_scales.reshape(blocks, hidden)
    up_piece = dequant_piece(
        lax.all_gather(code_up, "node", axis=0, tiled=True),
        lax.all_gather(scale_up, "node", axis=0, tiled=True),
    )
    pre = jnp.dot(rows_x, up_piece, preferred_element_type=jnp.float32)
    act = jax.nn.silu(pre).astype(jnp.bfloat16)
    factor = float(tok_dev * lax.axis_size("dp") * lax.axis_size("node")) ** (-0.5)
    second = contract_rows(rows_dy, act)
    rounded = (second * factor).astype(jnp.bfloat16)
    rounded = lax.optimization_barrier(rounded)
    grad_terms = rounded.astype(jnp.float32)
    partial_rows = lax.psum_scatter(
        grad_terms.astype(jnp.bfloat16), "node", scatter_dimension=0, tiled=True
    )
    result = lax.psum(partial_rows, "dp")
    return result[None]


def solution(mesh):
    in_specs = (
        P(("dp", "node", "local"), None),
        P(("dp", "node", "local"), None),
        P(("dp", "node", "local"), None),
        P("local", "node", None),
        P("local", "node", None),
    )
    out_specs = P("local", "node", None)
    return jax.shard_map(
        on_device, mesh=mesh, in_specs=in_specs, out_specs=out_specs, check_vma=False
    )
```

profile of v0, /device:TPU:0, one launch (start us, length us, event | category | flops | bytes accessed | tf_op | source)
XLA Modules:
  0.0 145.8 jit_solution(5696499167571732172)
XLA Ops:
  6.5 0.0 all-gather.3.cloned.1.call-start
  6.5 0.7 all-gather.3.cloned.1.call-update
  7.3 0.7 iota_compare_fusion
  8.0 1.2 reduce-window.6
  9.2 0.1 slice.12
  9.3 0.1 copy.10
  9.4 0.1 copy.11
  9.5 0.1 add_bitcast_fusion
  9.6 0.7 fusion.6
  10.3 0.7 compare_select_fusion
  11.0 2.6 %scatter_custom_fusion.1 = bf16[240,2048]{1,0:T(8,128)(2,1)S(1)} fusion(s32[192]{0:T(256)S(1)} %bitcast.31, bf16[192,2048]{1,0:T(8,128)(2,1)} %param.5, bf16[]{:T(256)} %constant.6.clone.1), kind=kCustom, calls=%fused_computation.5 | custom fusion | bytes 983552 | tf_op jit(solution)/shard_map/scatter | solution.py:18
  13.6 1.2 reshape.39
  14.8 4.3 %all-to-all-start.1 = ((bf16[4,60,2048]{2,1,0:T(8,128)(2,1)}), bf16[4,60,2048]{2,1,0:T(8,128)(2,1)S(1)}, u32[]{:S(2)}, u32[]{:S(2)}) async-start(bf16[4,60,2048]{2,1,0:T(8,128)(2,1)} %reshape.39), calls=%async_computation.1 | async-start | bytes 2097152 | tf_op jit(solution)/shard_map/all_to_all | solution.py:41
  19.0 2.6 %scatter_custom_fusion = bf16[240,2048]{1,0:T(8,128)(2,1)S(1)} fusion(s32[192]{0:T(256)S(1)} %bitcast.32, bf16[192,2048]{1,0:T(8,128)(2,1)} %param.6, bf16[]{:T(256)} %constant.6.clone.1), kind=kCustom, calls=%fused_computation.7 | custom fusion | bytes 983552 | tf_op jit(solution)/shard_map/scatter | solution.py:18
  21.7 0.0 copy-start
  21.7 1.2 reshape.37
  22.9 10.6 %all-to-all-done.1 = bf16[4,60,2048]{2,1,0:T(8,128)(2,1)S(1)} async-done(((bf16[4,60,2048]{2,1,0:T(8,128)(2,1)}), bf16[4,60,2048]{2,1,0:T(8,128)(2,1)S(1)}, u32[]{:S(2)}, u32[]{:S(2)}) %all-to-all-start.1) | async-done | bytes 983072 | tf_op jit(solution)/shard_map/all_to_all | solution.py:41
  33.5 3.5 %all-to-all-start = ((bf16[4,60,2048]{2,1,0:T(8,128)(2,1)}), bf16[4,60,2048]{2,1,0:T(8,128)(2,1)S(1)}, u32[]{:S(2)}, u32[]{:S(2)}) async-start(bf16[4,60,2048]{2,1,0:T(8,128)(2,1)} %reshape.37), calls=%async_computation | async-start | bytes 2097152 | tf_op jit(solution)/shard_map/all_to_all | solution.py:42
  37.0 0.0 reduce-scatter.2.cloned.1.call-start
  37.1 14.8 %all-gather = bf16[1,64,512]{2,1,0:T(8,128)(2,1)S(1)} all-gather(bf16[1,16,512]{2,1,0:T(8,128)(2,1)S(1)} %copy-done), channel_id=2, replica_groups=mesh['dp'=2,'node'=4,'local'=4] {'node'}, dimensions={1}, use_global_device_ids=true | all-gather | bytes 81920 | tf_op jit(solution)/shard_map/all_gather | solution.py:54
  51.8 0.2 reshape.40
  52.0 0.0 all-to-all-done
  52.0 1.2 reshape.38
  53.2 5.2 %all-gather.3.cloned.1.call-done = bf16[64,32,512]{2,1,0:T(8,128)(2,1)} async-done(((bf16[16,32,512]{2,1,0:T(8,128)(2,1)}), bf16[64,32,512]{2,1,0:T(8,128)(2,1)}) %all-gather.3.cloned.1.call-update) | async-done | bytes 2097168 | tf_op jit(solution)/shard_map/all_gather | solution.py:53
  58.4 2.2 %multiply_convert_fusion.1 = bf16[64,32,512]{2,1,0:T(8,128)(2,1)S(1)} fusion(bf16[64,32,512]{2,1,0:T(8,128)(2,1)} %all-gather.3.cloned.1.call-done, f32[64,512]{1,0:T(8,128)S(1)} %bitcast_convert_fusion), kind=kLoop, calls=%fused_computation.3 | loop fusion | flops 3145728 | bytes 4325376 | tf_op jit(solution)/shard_map/convert_element_type | solution.py:23
  60.6 4.0 %multiply_convert_fusion = bf16[2048,512]{1,0:T(8,128)(2,1)} fusion(bf16[240,2048]{1,0:T(8,128)(2,1)} %reshape.38, bf16[240,2048]{1,0:T(8,128)(2,1)S(1)} %reshape.40, bf16[2048,512]{1,0:T(8,128)(2,1)S(1)} %bitcast.23), kind=kOutput, calls=%fused_computation.2 | convolution fusion | flops 1009344512 | bytes 6160384 | tf_op jit(solution)/shard_map/dot_general | solution.py:27
  64.6 0.0 reduce-scatter.2.cloned.1.call-update
  64.6 0.0 all-reduce.3.cloned.1.call-start
  64.7 42.5 %reduce-scatter.2.cloned.1.call-done = bf16[512,512]{1,0:T(8,128)(2,1)} async-done(((bf16[2048,512]{1,0:T(8,128)(2,1)}), bf16[512,512]{1,0:T(8,128)(2,1)}) %reduce-scatter.2.cloned.1.call-update) | async-done | bytes 524304 | tf_op jit(solution)/shard_map/reduce_scatter | solution.py:63
  107.2 0.0 all-reduce.3.cloned.1.call-update
  107.2 30.2 %all-reduce.3.cloned.1.call-done = bf16[1,512,512]{2,1,0:T(8,128)(2,1)} async-done(((bf16[1,512,512]{2,1,0:T(8,128)(2,1)}), bf16[1,512,512]{2,1,0:T(8,128)(2,1)}) %all-reduce.3.cloned.1.call-update) | async-done | bytes 524304 | tf_op jit(solution)/shard_map/psum | solution.py:66
  137.4 1.9 %copy.16 = bf16[1,512,512]{2,1,0:T(8,128)(2,1)} copy(bf16[1,512,512]{2,1,0:T(8,128)(2,1)} %all-reduce.3.cloned.1.call-done) | data formatting | bytes 1048576
  (7 shorter events, 0.1 us)
Async XLA Ops:
  6.5 51.8 %all-gather.3.cloned.1.call-start = ((), (), s32[]{:S(2)}) async-start(), calls=%async_computation.3 | async-start | bytes 2621440 | tf_op jit(solution)/shard_map/all_gather | solution.py:53
  14.8 18.7 %all-to-all-start.1 = ((bf16[4,60,2048]{2,1,0:T(8,128)(2,1)}), bf16[4,60,2048]{2,1,0:T(8,128)(2,1)S(1)}, u32[]{:S(2)}, u32[]{:S(2)}) async-start(bf16[4,60,2048]{2,1,0:T(8,128)(2,1)} %reshape.39), calls=%async_computation.1 | async-start | bytes 2097152 | tf_op jit(solution)/shard_map/all_to_all | solution.py:41
  21.7 15.4 %copy-start = (bf16[1,16,512]{2,1,0:T(8,128)(2,1)S(1)}, bf16[1,16,512]{2,1,0:T(8,128)(2,1)}, u32[]{:S(2)}) copy-start(bf16[1,16,512]{2,1,0:T(8,128)(2,1)} %param.9) | copy-start | bytes 49156
  33.5 18.6 %all-to-all-start = ((bf16[4,60,2048]{2,1,0:T(8,128)(2,1)}), bf16[4,60,2048]{2,1,0:T(8,128)(2,1)S(1)}, u32[]{:S(2)}, u32[]{:S(2)}) async-start(bf16[4,60,2048]{2,1,0:T(8,128)(2,1)} %reshape.37), calls=%async_computation | async-start | bytes 2097152 | tf_op jit(solution)/shard_map/all_to_all | solution.py:42
  37.0 70.2 %reduce-scatter.2.cloned.1.call-start = ((), (), s32[]{:S(2)}) async-start(), calls=%async_computation.4 | async-start | bytes 2621440 | tf_op jit(solution)/shard_map/reduce_scatter | solution.py:63
  64.6 72.8 %all-reduce.3.cloned.1.call-start = ((), (), s32[]{:S(2)}) async-start(), calls=%async_computation.5 | async-start | bytes 1048576 | tf_op jit(solution)/shard_map/psum | solution.py:66
Sparse Core Ops, SparseCore 0:
  8.9 49.4 all-gather.2
  64.7 42.4 reduce-scatter.1
  109.5 27.8 all-reduce.2
where the time goes:
time: 146 us
  waiting for transfers between devices  89.2 us (61%)
  blocking collectives  14.8 us (10%)
  between operations  13.2 us (9%)
  local copies, waits for them, and re-layouts  11.1 us (8%)
  starting transfers between devices  7.87 us (5%)
  other arithmetic  5.63 us (4%)
  matrix products  4 us (3%)
    reduce_scatter x1, waiting for transfers between devices, on_device(): lax.psum_scatter(grad_terms.astype(jnp.bfloat16), 'node', scatter_dimensi...  42.5 us
    psum x1, waiting for transfers between devices, on_device(): result = lax.psum(partial_rows, 'dp')  30.2 us
    all_gather x1, blocking collectives, on_device(): lax.all_gather(scale_up, 'node', axis=0, tiled=True)  14.8 us
    all_to_all x1, waiting for transfers between devices, on_device(): lax.all_to_all(sent_x, 'local', split_axis=0, concat_axis=0, tiled=True)  10.6 us
    scatter x2, local copies, waits for them, and re-layouts, place(): blank_rows.at[slots].set(row_data)  5.25 us
    all_gather x1, waiting for transfers between devices, on_device(): lax.all_gather(code_up, 'node', axis=0, tiled=True)  5.17 us
    all_to_all x1, starting transfers between devices, on_device(): lax.all_to_all(sent_x, 'local', split_axis=0, concat_axis=0, tiled=True)  4.26 us
    dot_general x1, matrix products, contract_rows(): lax.dot_general(left_rows, right_rows, (((0,), (0,)), ((), ())), preferre...  4 us
  transfers between devices with their start and end apart: 5, of which 4 were waited for; matrix products, arithmetic and copies ran while one was open for 9% of the time, Pallas kernels for 0%

commit v1 on v0

--- a/solution.py
+++ b/solution.py
@@ -63,7 +63,7 @@
     partial_rows = lax.psum_scatter(
         grad_terms.astype(jnp.bfloat16), "node", scatter_dimension=0, tiled=True
     )
-    result = lax.psum(partial_rows, "dp")
+    result = jnp.sum(lax.all_gather(partial_rows, "dp"), axis=0)
     return result[None]
 
 

time: 146 us -> 139 us (0.952)
  waiting for transfers between devices: 89.2 us -> 81.1 us
  other arithmetic: 5.63 us -> 7.97 us
  local copies, waits for them, and re-layouts: 11.1 us -> 9.24 us
    psum x1 -> x0, waiting for transfers between devices: 30.2 us -> none  [on_device(): result = lax.psum(partial_rows, 'dp')]
    all_gather x0 -> x1, waiting for transfers between devices: none -> 22 us  [on_device(): result = jnp.sum(lax.all_gather(partial_rows, 'dp'), axis=0)]
    reduce_sum x0 -> x1, other arithmetic: none -> 2.35 us  [on_device(): result = jnp.sum(lax.all_gather(partial_rows, 'dp'), axis=0)]
    unnamed x4 -> x3, local copies, waits for them, and re-layouts: 1.88 us -> 0.01 us
where the time goes in v1:
time: 139 us; the launch traced here: 138 us
  waiting for transfers between devices  81.1 us (58%)
  blocking collectives  14.8 us (11%)
  between operations  13.2 us (9%)
  local copies, waits for them, and re-layouts  9.24 us (7%)
  other arithmetic  7.97 us (6%)
  starting transfers between devices  7.87 us (6%)
  matrix products  4 us (3%)
    reduce_scatter x1, waiting for transfers between devices, on_device(): lax.psum_scatter(grad_terms.astype(jnp.bfloat16), 'node', scatter_dimensi...  42.5 us
    all_gather x1, waiting for transfers between devices, on_device(): result = jnp.sum(lax.all_gather(partial_rows, 'dp'), axis=0)  22 us
    all_gather x1, blocking collectives, on_device(): lax.all_gather(scale_up, 'node', axis=0, tiled=True)  14.8 us
    all_to_all x1, waiting for transfers between devices, on_device(): lax.all_to_all(sent_x, 'local', split_axis=0, concat_axis=0, tiled=True)  10.6 us
    scatter x2, local copies, waits for them, and re-layouts, place(): blank_rows.at[slots].set(row_data)  5.25 us
    all_gather x1, waiting for transfers between devices, on_device(): lax.all_gather(code_up, 'node', axis=0, tiled=True)  5.17 us
    all_to_all x1, starting transfers between devices, on_device(): lax.all_to_all(sent_x, 'local', split_axis=0, concat_axis=0, tiled=True)  4.26 us
    dot_general x1, matrix products, contract_rows(): lax.dot_general(left_rows, right_rows, (((0,), (0,)), ((), ())), preferre...  4 us
  transfers between devices with their start and end apart: 5, of which 4 were waited for; matrix products, arithmetic and copies ran while one was open for 9% of the time, Pallas kernels for 0%

profile of v1, /device:TPU:0, one launch (start us, length us, event | category | flops | bytes accessed | tf_op | source)
XLA Modules:
  0.0 138.1 jit_solution(1387920841038282267)
XLA Ops:
  6.5 0.0 all-gather.5.cloned.1.call-start
  6.5 0.7 all-gather.5.cloned.1.call-update
  7.3 0.7 iota_compare_fusion
  8.0 1.2 reduce-window.6
  9.2 0.1 slice.12
  9.3 0.1 copy.10
  9.4 0.1 copy.11
  9.5 0.1 add_bitcast_fusion
  9.6 0.7 fusion.6
  10.3 0.7 compare_select_fusion
  11.0 2.6 %scatter_custom_fusion.1 = bf16[240,2048]{1,0:T(8,128)(2,1)S(1)} fusion(s32[192]{0:T(256)S(1)} %bitcast.32, bf16[192,2048]{1,0:T(8,128)(2,1)} %param.5, bf16[]{:T(256)} %constant.8.clone.1), kind=kCustom, calls=%fused_computation.5 | custom fusion | bytes 983552 | tf_op jit(solution)/shard_map/scatter | solution.py:18
  13.6 1.2 reshape.39
  14.8 4.3 %all-to-all-start.1 = ((bf16[4,60,2048]{2,1,0:T(8,128)(2,1)}), bf16[4,60,2048]{2,1,0:T(8,128)(2,1)S(1)}, u32[]{:S(2)}, u32[]{:S(2)}) async-start(bf16[4,60,2048]{2,1,0:T(8,128)(2,1)} %reshape.39), calls=%async_computation.1 | async-start | bytes 2097152 | tf_op jit(solution)/shard_map/all_to_all | solution.py:41
  19.0 2.6 %scatter_custom_fusion = bf16[240,2048]{1,0:T(8,128)(2,1)S(1)} fusion(s32[192]{0:T(256)S(1)} %bitcast.33, bf16[192,2048]{1,0:T(8,128)(2,1)} %param.6, bf16[]{:T(256)} %constant.8.clone.1), kind=kCustom, calls=%fused_computation.7 | custom fusion | bytes 983552 | tf_op jit(solution)/shard_map/scatter | solution.py:18
  21.7 0.0 copy-start
  21.7 1.2 reshape.37
  22.9 10.6 %all-to-all-done.1 = bf16[4,60,2048]{2,1,0:T(8,128)(2,1)S(1)} async-done(((bf16[4,60,2048]{2,1,0:T(8,128)(2,1)}), bf16[4,60,2048]{2,1,0:T(8,128)(2,1)S(1)}, u32[]{:S(2)}, u32[]{:S(2)}) %all-to-all-start.1) | async-done | bytes 983072 | tf_op jit(solution)/shard_map/all_to_all | solution.py:41
  33.5 3.5 %all-to-all-start = ((bf16[4,60,2048]{2,1,0:T(8,128)(2,1)}), bf16[4,60,2048]{2,1,0:T(8,128)(2,1)S(1)}, u32[]{:S(2)}, u32[]{:S(2)}) async-start(bf16[4,60,2048]{2,1,0:T(8,128)(2,1)} %reshape.37), calls=%async_computation | async-start | bytes 2097152 | tf_op jit(solution)/shard_map/all_to_all | solution.py:42
  37.0 0.0 reduce-scatter.2.cloned.1.call-start
  37.1 14.8 %all-gather = bf16[1,64,512]{2,1,0:T(8,128)(2,1)S(1)} all-gather(bf16[1,16,512]{2,1,0:T(8,128)(2,1)S(1)} %copy-done), channel_id=2, replica_groups=mesh['dp'=2,'node'=4,'local'=4] {'node'}, dimensions={1}, use_global_device_ids=true | all-gather | bytes 81920 | tf_op jit(solution)/shard_map/all_gather | solution.py:54
  51.8 0.2 reshape.40
  52.0 0.0 all-to-all-done
  52.0 1.2 reshape.38
  53.2 5.2 %all-gather.5.cloned.1.call-done = bf16[64,32,512]{2,1,0:T(8,128)(2,1)} async-done(((bf16[16,32,512]{2,1,0:T(8,128)(2,1)}), bf16[64,32,512]{2,1,0:T(8,128)(2,1)}) %all-gather.5.cloned.1.call-update) | async-done | bytes 2097168 | tf_op jit(solution)/shard_map/all_gather | solution.py:53
  58.4 2.2 %multiply_convert_fusion.1 = bf16[64,32,512]{2,1,0:T(8,128)(2,1)S(1)} fusion(bf16[64,32,512]{2,1,0:T(8,128)(2,1)} %all-gather.5.cloned.1.call-done, f32[64,512]{1,0:T(8,128)S(1)} %bitcast_convert_fusion), kind=kLoop, calls=%fused_computation.3 | loop fusion | flops 3145728 | bytes 4325376 | tf_op jit(solution)/shard_map/convert_element_type | solution.py:23
  60.6 4.0 %multiply_convert_fusion = bf16[2048,512]{1,0:T(8,128)(2,1)} fusion(bf16[240,2048]{1,0:T(8,128)(2,1)} %reshape.38, bf16[240,2048]{1,0:T(8,128)(2,1)S(1)} %reshape.40, bf16[2048,512]{1,0:T(8,128)(2,1)S(1)} %bitcast.24), kind=kOutput, calls=%fused_computation.2 | convolution fusion | flops 1009344512 | bytes 6160384 | tf_op jit(solution)/shard_map/dot_general | solution.py:27
  64.6 0.0 reduce-scatter.2.cloned.1.call-update
  64.6 0.0 all-gather.7.cloned.1.call-start
  64.7 42.5 %reduce-scatter.2.cloned.1.call-done = bf16[512,512]{1,0:T(8,128)(2,1)} async-done(((bf16[2048,512]{1,0:T(8,128)(2,1)}), bf16[512,512]{1,0:T(8,128)(2,1)}) %reduce-scatter.2.cloned.1.call-update) | async-done | bytes 524304 | tf_op jit(solution)/shard_map/reduce_scatter | solution.py:63
  107.2 0.0 all-gather.7.cloned.1.call-update
  107.2 22.0 %all-gather.7.cloned.1.call-done = bf16[1024,512]{1,0:T(8,128)(2,1)} async-done(((bf16[512,512]{1,0:T(8,128)(2,1)}), bf16[1024,512]{1,0:T(8,128)(2,1)}) %all-gather.7.cloned.1.call-update) | async-done | bytes 1048592 | tf_op jit(solution)/shard_map/all_gather | solution.py:66
  129.2 2.3 %reduce_sum.25 = bf16[512,512]{1,0:T(8,128)(2,1)} reduce(bf16[2,512,512]{2,1,0:T(8,128)(2,1)} %bitcast.25, bf16[]{:T(256)} %constant.8.clone.1), dimensions={0}, to_apply=%region_6.7 | reduce | flops 262144 | bytes 1572866 | tf_op jit(solution)/shard_map/reduce_sum | solution.py:66
  (7 shorter events, 0.1 us)
Async XLA Ops:
  6.5 51.8 %all-gather.5.cloned.1.call-start = ((), (), s32[]{:S(2)}) async-start(), calls=%async_computation.3 | async-start | bytes 2621440 | tf_op jit(solution)/shard_map/all_gather | solution.py:53
  14.8 18.7 %all-to-all-start.1 = ((bf16[4,60,2048]{2,1,0:T(8,128)(2,1)}), bf16[4,60,2048]{2,1,0:T(8,128)(2,1)S(1)}, u32[]{:S(2)}, u32[]{:S(2)}) async-start(bf16[4,60,2048]{2,1,0:T(8,128)(2,1)} %reshape.39), calls=%async_computation.1 | async-start | bytes 2097152 | tf_op jit(solution)/shard_map/all_to_all | solution.py:41
  21.7 15.4 %copy-start = (bf16[1,16,512]{2,1,0:T(8,128)(2,1)S(1)}, bf16[1,16,512]{2,1,0:T(8,128)(2,1)}, u32[]{:S(2)}) copy-start(bf16[1,16,512]{2,1,0:T(8,128)(2,1)} %param.9) | copy-start | bytes 49156
  33.5 18.6 %all-to-all-start = ((bf16[4,60,2048]{2,1,0:T(8,128)(2,1)}), bf16[4,60,2048]{2,1,0:T(8,128)(2,1)S(1)}, u32[]{:S(2)}, u32[]{:S(2)}) async-start(bf16[4,60,2048]{2,1,0:T(8,128)(2,1)} %reshape.37), calls=%async_computation | async-start | bytes 2097152 | tf_op jit(solution)/shard_map/all_to_all | solution.py:42
  37.0 70.2 %reduce-scatter.2.cloned.1.call-start = ((), (), s32[]{:S(2)}) async-start(), calls=%async_computation.4 | async-start | bytes 2621440 | tf_op jit(solution)/shard_map/reduce_scatter | solution.py:63
  64.6 64.6 %all-gather.7.cloned.1.call-start = ((), (), s32[]{:S(2)}) async-start(), calls=%async_computation.5 | async-start | bytes 1572864 | tf_op jit(solution)/shard_map/all_gather | solution.py:66
Sparse Core Ops, SparseCore 0:
  8.9 49.4 all-gather.4
  64.7 42.4 reduce-scatter.1
  108.7 20.4 all-gather.6
